TPU v7x, 32 devices: a whole 2x2x4 slice. The times are simulated.
32 devices in a mesh: dom: 16 (over z, y, core), feat: 2 (over x).
Axes of the slice: x: 2, y: 2, z: 4, core: 2. Of those that a mesh axis runs over, the one named last changes fastest.
Arguments:
- features: bfloat16 [256, 8192], P('feat', 'dom'), may hold values from -6 to 6
- in_degree: int32 [8192], P('dom'), may hold values from 16 to 64
- send_rows: int32 [16, 16, 16], P('dom'), may hold values from 0 to 511
- send_count: int32 [16, 16], P('dom'), may hold values from 0 to 16, as said below
- hub_owner: int32 [4], replicated, may hold values from 0 to 15, as said below
- hub_rows: int32 [4, 128], replicated, may hold values from 0 to 511
- local_dest: int32 [256], P('dom'), may hold values from 0 to 3
- local_source: int32 [256], P('dom'), may hold values from 0 to 3
- local_tiles: bfloat16 [256, 128, 128], P('dom'), may hold values from 0 to 1
- border_dest: int32 [256], P('dom'), may hold values from 0 to 3
- border_source: int32 [256], P('dom'), may hold values from 0 to 1
- border_tiles: bfloat16 [256, 128, 128], P('dom'), may hold values from 0 to 1
- hub_dest: int32 [256], P('dom'), may hold values from 0 to 3
- hub_source: int32 [256], P('dom'), may hold values from 0 to 3
- hub_tiles: bfloat16 [256, 128, 128], P('dom'), may hold values from 0 to 1
- self_weight: bfloat16 [256, 256], P('feat'), may hold values from -0.375 to 0.375
- neighbor_weight: bfloat16 [256, 256], P('feat'), may hold values from -0.375 to 0.375
- out_bias: float32 [256], P('feat'), may hold values from -3 to 3
Outputs:
- updated: bfloat16 [256, 8192], P('feat', 'dom')
Inputs may be any that keep to these rules, and one draw needn't show every extreme that they name: send_count[q, p] of the 16 slots from q to p are live; in every draw some destinations receive 16 live rows from every source. Hub block b belongs to partition hub_owner[b]; one partition owns exactly 2 blocks, every other partition at most one.
All inputs are finite; a program needn't handle non-finite values.
Results may differ from a plain program's by a relative error of at most 0.0034.
Values may be sent and summed in bfloat16 or wider, within the bound.
No kernel may reach another device: no remote copies, remote signals or barrier semaphores. Data moves between devices by JAX's collectives and lax.ppermute only.
A program may use at most 64 MiB of HBM per device.

v0:
```python
import functools

import jax
import jax.numpy as jnp
from jax import lax
from jax.experimental import pallas as pl
from jax.experimental.pallas import tpu as pltpu
from jax.sharding import PartitionSpec as P

BF16 = jnp.bfloat16
F32 = jnp.float32
VM = pl.BlockSpec(memory_space=pltpu.VMEM)
SM = pl.BlockSpec(memory_space=pltpu.SMEM)
ANY = pl.BlockSpec(memory_space=pl.ANY)
HBM = pl.BlockSpec(memory_space=pltpu.HBM)
LAST = (((1,), (1,)), ((), ()))
FIRST_LAST = (((0,), (1,)), ((), ()))


def call(body, outs, specs, scratch=(), flops=0, size=0, name=None, room=8 << 20):
    return pl.pallas_call(
        body,
        out_shape=outs,
        in_specs=specs,
        out_specs=jax.tree.map(lambda out: SM if out.dtype == jnp.int32 else VM, outs),
        scratch_shapes=scratch,
        compiler_params=pltpu.CompilerParams(vmem_limit_bytes=room),
        cost_estimate=pl.CostEstimate(flops=flops, bytes_accessed=size, transcendentals=0),
        name=name,
    )


def dot(a, b, contract=(((1,), (0,)), ((), ()))):
    return lax.dot_general(a, b, contract, preferred_element_type=F32)


def rows(start, size):
    return pl.ds(pl.multiple_of(start, size), size)


def line_of(place):
    for shift in (8, 4, 2, 1):
        place = place ^ (place >> shift)
    return place & 1


def order(line, bits):
    down = list(range(bits))[::-1]
    return down if line else down[-1:] + down[:-1]


def turned(chip, line, bits):
    return sum(((chip >> b) & 1) << i for i, b in enumerate(order(line, bits)))


def relative_chip(place, line, bits):
    chips = [turned(place >> 1, each, bits) for each in (0, 1)]
    return chips[0] + (chips[1] - chips[0]) * line


def relative(place, bits):
    line = line_of(place)
    return 2 * relative_chip(place, line, bits) + line


def assignments(blocks):
    if blocks != 4:
        return [[(b & 1, b >> 1) for b in range(blocks)]]
    ways = []
    for mate in (1, 2, 3):
        first = [0, mate]
        second = [b for b in range(4) if b not in first]
        for lines in ((first, second), (second, first)):
            ways.append([(int(b in lines[1]), lines[int(b in lines[1])].index(b)) for b in range(4)])
    return ways


def assign(owner, blocks, parts):
    bits = parts.bit_length() - 2
    chips = [[turned(owner[b] >> 1, line, bits) for b in range(blocks)] for line in (0, 1)]
    best = None
    for way in assignments(blocks):
        least = jnp.int32(parts - 1)
        for b in range(blocks):
            for other in range(b):
                if way[b][0] == way[other][0]:
                    apart = chips[way[b][0]][b] ^ chips[way[b][0]][other]
                    least = jnp.minimum(least, apart)
        level = sum((least >> i > 0).astype(jnp.int32) for i in range(bits))
        if best is None:
            best = level, [(jnp.int32(line), jnp.int32(slot)) for line, slot in way]
        else:
            better = level > best[0]
            best = jnp.maximum(level, best[0]), [
                (jnp.where(better, line, old), jnp.where(better, slot, place))
                for (line, slot), (old, place) in zip(way, best[1])
            ]
    return best


def partners(parts, k):
    if k == 0:
        return [(i, i ^ 1) for i in range(parts)]
    bits = parts.bit_length() - 2
    place = {relative(i, bits): i for i in range(parts)}
    return [(i, place[relative(i, bits) ^ (1 << k)]) for i in range(parts)]


def column(row):
    m = row.shape[1]
    down = lax.broadcasted_iota(jnp.int32, (m, m), 0)
    across = lax.broadcasted_iota(jnp.int32, (m, m), 1)
    return jnp.sum(jnp.where(down == across, row, jnp.zeros_like(row)), axis=1, keepdims=True)


def fetch(pairs, sems):
    copies = [pltpu.make_async_copy(a, b, sems.at[i]) for i, (a, b) in enumerate(pairs)]
    for copy in copies:
        copy.start()
    return copies


def prepare(lists_size, *refs):
    inputs, outs, scratch = refs[:18], refs[18:-14], refs[-14:]
    choice, marks, level, self_weight, bias = outs[:5]
    averages, parts_out = outs[5:11], outs[11:]
    owner, lists, count, hubs, weight, features, places, degree, *rest = scratch
    dests, sources, tiles, near, far, sems = rest
    landing = [owner, lists, count, hubs]
    landing += [ref.at[i] for i in range(3) for ref in (dests, sources, tiles)]
    landing += [degree, features, weight, self_weight, bias]
    copies = [
        pltpu.make_async_copy(a, b, sems.at[i]) for i, (a, b) in enumerate(zip(inputs, landing))
    ]
    for copy in copies:
        copy.start()
    for copy in copies[:4]:
        copy.wait()
    me = lax.axis_index("dom")
    line = line_of(me)
    parts, cap = lists.shape[1:]
    blocks, tile = hubs.shape
    vertices = choice.shape[1]
    pairs = (blocks + 1) // 2
    border, half = parts * cap // 2, parts * cap // 2 + pairs * tile
    shape = (parts, cap, cap)
    slot = lax.broadcasted_iota(jnp.int32, shape, 1)
    across = lax.broadcasted_iota(jnp.int32, shape, 2)
    index = jnp.sum(jnp.where(slot == across, lists[0][:, None, :], 0), axis=2, keepdims=True)
    shape = (parts, cap, parts)
    target = lax.broadcasted_iota(jnp.int32, shape, 0)
    across = lax.broadcasted_iota(jnp.int32, shape, 2)
    live = jnp.sum(jnp.where(target == across, count[...][None], 0), axis=2, keepdims=True)
    slot = lax.broadcasted_iota(jnp.int32, (parts, cap, 1), 1)
    index = jnp.where(slot < live, index, -1)

    def onehot(index):
        vertex = lax.broadcasted_iota(jnp.int32, (index.shape[0], vertices), 1)
        return (vertex == index).astype(F32).astype(BF16)

    for part in range(parts):
        stays = 1 - (line_of(part) ^ line)
        place = turned(part >> 1, line_of(part), parts.bit_length() - 2)
        choice[pl.ds(pl.multiple_of(stays * half + place * cap, cap), cap), :] = onehot(index[part])
    short, places_of = assign(owner, blocks, parts)
    level[0] = short
    if blocks % 2:
        odd = pl.ds(pl.multiple_of(line * half + border + (pairs - 1) * tile, cap), tile)
        choice[odd, :] = jnp.zeros((tile, vertices), BF16)
    for b, (its_line, slot) in enumerate(places_of):
        stays = 1 - (its_line ^ line)
        there = pl.ds(pl.multiple_of(stays * half + border + slot * tile, cap), tile)
        mine = jnp.where(owner[b] == me, hubs[b : b + 1, :], -1)
        choice[there, :] = onehot(column(mine))
        places[b] = lists_size + slot + (its_line ^ line) * pairs
    bits = parts.bit_length() - 2
    mine = relative(me, bits) >> 1
    marks[...] = jnp.zeros_like(marks)
    for b, (its_line, slot) in enumerate(places_of):
        owned = relative_chip(owner[b], line, bits)
        for k in range(bits):
            here = (its_line == line) & (((mine >> k) ^ 1) == (owned >> k))
            row = pl.ds(k * pairs + slot, 1)
            marks[row, :] = marks[row, :] + jnp.where(here, 1.0, 0.0)
    sum_tiles(
        copies[4:14], places, dests, sources, tiles, degree, near, far, averages
    )
    for copy in copies[14:]:
        copy.wait()
    if parts_out:
        known, ahead, begun = parts_out
        width = features.shape[0]
        place = lax.axis_index("feat")
        known[...] = dot(weight[:, rows(place * width, width)], features[...])
        ahead[...] = weight[:, rows((1 - place) * width, width)]
        begun[...] = dot(self_weight[:, rows(place * width, width)], features[...]) + column(
            bias[...]
        )


def sum_tiles(copies, places, dests, sources, tiles, degree, near, far, averages):
    count, tile = tiles.shape[1:3]
    near[...] = jnp.zeros_like(near)
    far[...] = jnp.zeros_like(far)
    for i in range(3):
        for copy in copies[3 * i : 3 * i + 3]:
            copy.wait()
        sums = far if i else near
        for t in range(count):
            source = places[sources[i, t]] if i == 2 else sources[i, t]
            there = (rows(dests[i, t] * tile, tile), rows(source * tile, tile))
            sums[there] = sums[there] + tiles[i, t].astype(F32)
    copies[9].wait()
    for r in range(near.shape[0] // tile):
        there = slice(r * tile, (r + 1) * tile)
        below = column(degree[:, there].astype(F32))
        known = averages[2].shape[1]
        for sums, high, low in ((near[there, :], *averages[:2]), (far[there, :known], *averages[2:4])):
            mean = sums / below
            top = mean.astype(BF16)
            high[there, :] = top
            low[there, :] = (mean - top.astype(F32)).astype(BF16)
        mean = (far[there, known:] / below).T
        top = mean.astype(BF16)
        averages[4][:, there] = top
        averages[5][:, there] = (mean - top.astype(F32)).astype(BF16)


def pick(weight, features, choice, *refs):
    *known, _, projected, message = refs
    total = dot(weight[...], features[...])
    if known:
        total = total + known[0][...]
    projected[...] = total.astype(BF16)
    message[...] = dot(
        choice[: message.shape[0], :], total.astype(BF16), LAST
    ).astype(BF16)


def remain(projected, choice, kept):
    kept[...] = dot(choice[kept.shape[0] :, :], projected[...], LAST).astype(BF16)


def step(k, parts, cap, last, short, shorten, keep, hub, received, marks, _, *outs):
    bits = parts.bit_length() - 2
    me = relative(lax.axis_index("dom"), bits)
    bit = (me >> k) & 1
    border = parts * cap // 2
    size = outs[1].shape[0] if last else outs[2].shape[0]
    held = hub[hub.shape[0] - size :, :]
    if short:
        tile = received.shape[0] - border
        arrived = received[border:, :].astype(F32)
        pairs = size // tile
        merged = jnp.concatenate(
            [
                held[i * tile : (i + 1) * tile]
                + (arrived * marks[(k - 1) * pairs + i : (k - 1) * pairs + i + 1, :]).astype(BF16)
                for i in range(pairs)
            ],
            axis=0,
        )
    else:
        merged = held + received[border:, :]
    run = (1 << k) * cap
    first, second = outs[:2]
    if last:
        for group in range(parts // 2):
            here = slice(group * cap, (group + 1) * cap)
            chips = [
                sum(((group >> (i + 1)) & 1) << b for i, b in enumerate(order(line, bits)))
                for line in (0, 1)
            ]
            for top, values in ((bit, keep), (1 - bit, received)):
                origin = jnp.where(
                    (me & 1) == 1,
                    chips[1] + (top << order(1, bits)[-1]),
                    chips[0] + (top << order(0, bits)[-1]),
                )
                place = 2 * origin + (line_of(group) ^ top)
                first[rows(place * cap, cap), :] = values[here, :]
        first[2 * border :, :] = merged
        second[...] = merged
        return
    ahead = (me >> (k + 1)) & 1
    for pair in range(parts >> (k + 2)):
        stay, go = rows((2 * pair + ahead) * run, run), rows((2 * pair + 1 - ahead) * run, run)
        mine, theirs = rows((2 * pair + bit) * run, run), rows((2 * pair + 1 - bit) * run, run)
        first[mine, :] = keep[stay, :]
        first[theirs, :] = received[stay, :]
        second[mine, :] = keep[go, :]
        second[theirs, :] = received[go, :]
    outs[2][...] = merged
    brief = outs[3] if shorten is None else second
    if shorten is None:
        second[border:, :] = merged
        brief[:border, :] = second[:border, :]
    if shorten is False:
        second[border:, :] = merged
    else:
        tile = brief.shape[0] - border
        pairs = size // tile
        brief[border:, :] = sum(merged[i * tile : (i + 1) * tile] for i in range(pairs))


def own_terms(local_high, local_low, projected, weight, begun, features, total):
    width = features.shape[0]
    if begun.shape[0] == 1:
        rest = dot(weight[...], features[...]) + column(begun[...])
    else:
        place = lax.axis_index("feat")
        rest = begun[...] + dot(weight[:, rows((1 - place) * width, width)], features[...])
    total[...] = (
        rest
        + dot(projected[...], local_high[...], LAST)
        + dot(projected[...], local_low[...], LAST)
    )


def far_terms(high, low, near, before, total):
    total[...] = (
        before[...]
        + dot(near[...], high[...], FIRST_LAST)
        + dot(near[...], low[...], FIRST_LAST)
    )


def finish(high, low, theirs, before, updated):
    arrived = theirs[...].T
    total = before[...] + dot(arrived, high[...]) + dot(arrived, low[...])
    updated[...] = jnp.maximum(total, 0.0).astype(BF16)


def shards(
    features, in_degree, send_rows, send_count, hub_owner, hub_rows,
    local_dest, local_source, local_tiles, border_dest, border_source, border_tiles,
    hub_dest, hub_source, hub_tiles, self_weight, neighbor_weight, out_bias,
):
    vertices = features.shape[1]
    count, tile, _ = local_tiles.shape
    width = self_weight.shape[0]
    parts, feats = lax.axis_size("dom"), lax.axis_size("feat")
    cap = send_rows.shape[2]
    blocks = hub_owner.shape[0]
    steps = parts.bit_length() - 1
    pairs = (blocks + 1) // 2
    border, hub = parts * cap // 2, pairs * tile
    near_size, far_size = vertices, 2 * border + 2 * hub

    def like(*shape, kind=BF16):
        return jax.ShapeDtypeStruct(shape, kind)

    def swap(x, k):
        return lax.ppermute(x, "dom", partners(parts, k))

    if feats == 2:
        feature_blocks = [features, lax.ppermute(features, "feat", [(0, 1), (1, 0)])]
    else:
        feature_blocks = [lax.all_gather(features, "feat", axis=0, tiled=True)]
    fixed = [
        pltpu.with_memory_space_constraint(x, pltpu.HBM)
        for x in (
            hub_owner, send_rows, send_count, hub_rows,
            local_dest, local_source, local_tiles, border_dest, border_source, border_tiles,
            hub_dest, hub_source, hub_tiles, in_degree.reshape(1, vertices),
            features, neighbor_weight, self_weight, out_bias.reshape(1, width),
        )
    ]
    early = ()
    if feats == 2:
        early = (
            like(width, vertices, kind=F32),
            like(width, features.shape[0]),
            like(width, vertices, kind=F32),
        )
    choice, marks, level, near_weight, bias, *averages = call(
        functools.partial(prepare, 2 * border // tile),
        (
            like(2 * (border + hub), vertices),
            like((steps - 1) * pairs, width, kind=F32),
            like(1, kind=jnp.int32),
            like(*self_weight.shape),
            like(1, width, kind=F32),
            *(like(vertices, near_size),) * 2,
            *(like(vertices, far_size - hub),) * 2,
            *(like(hub, vertices),) * 2,
            *early,
        ),
        [HBM] * 18,
        [
            pltpu.SMEM(hub_owner.shape, jnp.int32),
            pltpu.VMEM(send_rows.shape, jnp.int32),
            pltpu.VMEM(send_count.shape, jnp.int32),
            pltpu.VMEM(hub_rows.shape, jnp.int32),
            pltpu.VMEM(neighbor_weight.shape, BF16),
            pltpu.VMEM(features.shape, BF16),
            pltpu.SMEM(hub_owner.shape, jnp.int32),
            pltpu.VMEM((1, vertices), jnp.int32),
            pltpu.SMEM((3, count), jnp.int32),
            pltpu.SMEM((3, count), jnp.int32),
            pltpu.VMEM((3, count, tile, tile), BF16),
            pltpu.VMEM((vertices, near_size), F32),
            pltpu.VMEM((vertices, far_size), F32),
            pltpu.SemaphoreType.DMA((18,)),
        ],
        size=8 << 20, name="prepare", room=(8 << 20) + 8 * vertices * (near_size + far_size),
    )(*fixed)
    local_high, local_low, far_high, far_low, late_high, late_low, *early = averages
    weight, known = (early[1], early[:1]) if early else (neighbor_weight, [])
    projected, message = call(
        pick, (like(width, vertices), like(border + hub, width)),
        [VM] * (3 + len(known)) + [ANY], size=1 << 20, name="pick",
    )(weight, feature_blocks[-1], choice, *known, marks)
    received = swap(message, 0)
    kept = call(
        remain, like(border + hub, width), [VM] * 2, size=1 << 20, name="remain"
    )(projected, choice)
    begun = early[2] if early else bias
    own = functools.partial(
        call(
            own_terms, like(width, vertices, kind=F32), [VM] * 6,
            flops=4 * vertices * width * (near_size + width), size=2 << 20, name="own",
        ),
        local_high, local_low, projected, near_weight, begun, feature_blocks[-1],
    )
    keep, message, held, brief = call(
        functools.partial(step, 0, parts, cap, False, False, None),
        (like(border, width), like(border + hub, width), like(hub, width), like(border + tile, width)),
        [VM] * 4 + [ANY], name="step0",
    )(kept, kept, received, marks, marks)

    def chain(level, keep, message, held, brief, marks):
        for k in range(1, steps):
            received = swap(brief if k == 1 <= level else message, k)
            last, shorten = k == steps - 1, k + 1 <= level
            outs = (
                (like(2 * border + hub, width), like(hub, width))
                if last
                else (
                    like(border, width),
                    like(border + (tile if shorten else hub), width),
                    like(hub, width),
                )
            )
            keep, message, *rest = call(
                functools.partial(step, k, parts, cap, last, k <= level, shorten),
                outs, [VM] * 4 + [ANY], name=f"step{k}_{level}",
            )(keep, held, received, marks, marks)
            held = rest[0] if rest else None
        return keep, message

    keep, message = lax.switch(
        level[0],
        [functools.partial(chain, level) for level in range(steps)],
        keep, message, held, brief, marks,
    )
    theirs = swap(message, 0)
    total = own()
    total = call(
        far_terms, like(width, vertices, kind=F32), [VM] * 4,
        flops=4 * vertices * width * (far_size - hub), size=2 << 20, name="far",
    )(far_high, far_low, keep, total)
    return call(finish, like(width, vertices), [VM] * 4, size=1 << 20, name="finish")(
        late_high, late_low, theirs, total
    )


def solution(mesh):
    dom, feat = P("dom"), P("feat")
    whole = P("dom", None, None)
    placed = (
        P("feat", "dom"), dom, whole, P("dom", None), P(), P(),
        dom, dom, whole, dom, dom, whole, dom, dom, whole,
        P("feat", None), P("feat", None), feat,
    )
    return jax.shard_map(
        shards, mesh=mesh, in_specs=placed, out_specs=P("feat", "dom"), check_vma=False
    )
```

profile of v0, /device:TPU:0, one launch (start us, length us, event | category | flops | bytes accessed | tf_op | source)
XLA Modules:
  0.0 25.2 jit_solution(3355554406754401320)
XLA Ops:
  0.0 2.9 %collective-permute-start.12 = (bf16[128,512]{1,0:T(8,128)(2,1)}, bf16[128,512]{1,0:T(8,128)(2,1)S(1)}, u32[]{:S(2)}, u32[]{:S(2)}) collective-permute-start(bf16[128,512]{1,0:T(8,128)(2,1)} %refs_14_.1), channel_id=1, source_target_pairs={{0,1},{1,0},{2,3},{3,2},{4,5},{5,4},{6,7},{7,6},{8,9},{9,8},{10,11... | collective-permute-start | bytes 393224 | tf_op jit(solution)/shard_map/ppermute | solution.py:357
  2.9 3.1 %prepare.1 = (bf16[768,512]{1,0:T(8,128)(2,1)S(1)}, f32[6,128]{1,0:T(8,128)S(1)}, s32[1]{0:T(128)}, bf16[128,256]{1,0:T(8,128)(2,1)S(1)}, f32[1,128]{1,0:T(1,128...) custom-call(s32[4]{0:T(128)} %refs_0_.1, ...), custom_call_target="tpu_custom_call" | custom-call | bytes 8388608 | tf_op jit(solution)/shard_map/prepare/pallas_call | solution.py:376
  6.0 0.6 %collective-permute-done.12.features = bf16[128,512]{1,0:T(8,128)(2,1)S(1)} collective-permute-done((bf16[128,512]{1,0:T(8,128)(2,1)}, bf16[128,512]{1,0:T(8,128)(2,1)S(1)}, u32[]{:S(2)}, u32[]{:S(2)}) %collective-permute-start.12) | collective-permute-done | bytes 131104 | tf_op jit(solution)/shard_map/ppermute | solution.py:357
  6.6 0.4 %pick.1 = (bf16[128,512]{1,0:T(8,128)(2,1)S(1)}, bf16[384,128]{1,0:T(8,128)(2,1)S(1)}) custom-call(bf16[128,128]{1,0:T(8,128)(2,1)S(1)} %get-tuple-element.101.weight, bf16[128,512]{1,0:T(8,128)(2,1)S(1)} %collective-permute-done.12.features, bf16[768,512]{1,0:T(8,128)(2,1)S(1)} %get-tuple-element.102.choice, f32[128,512]{1,0:T(8,128)S(1)} %get-tuple-element.103.refs_0_, ...), custom_call_target="tpu_custom_call" | custom-call | bytes 1048576 | tf_op jit(solution)/shard_map/pick/pallas_call | solution.py:410
  7.0 0.1 collective-permute-start.13
  7.8 0.3 %remain.1.keep.hub = bf16[384,128]{1,0:T(8,128)(2,1)S(1)} custom-call(bf16[128,512]{1,0:T(8,128)(2,1)S(1)} %get-tuple-element.105.projected, bf16[768,512]{1,0:T(8,128)(2,1)S(1)} %get-tuple-element.102.choice), custom_call_target="tpu_custom_call" | custom-call | bytes 1048576 | tf_op jit(solution)/shard_map/remain/pallas_call | solution.py:415
  8.0 0.4 %collective-permute-done.13.received = bf16[384,128]{1,0:T(8,128)(2,1)S(1)} collective-permute-done((bf16[384,128]{1,0:T(8,128)(2,1)S(1)}, bf16[384,128]{1,0:T(8,128)(2,1)S(1)}, u32[]{:S(2)}, u32[]{:S(2)}) %collective-permute-start.13) | collective-permute-done | bytes 98336 | tf_op jit(solution)/shard_map/ppermute | solution.py:354
  8.4 0.1 step0.1
  8.5 14.1 %conditional.1 = ((bf16[512,128]{1,0:T(8,128)(2,1)S(1)}, bf16[256,128]{1,0:T(8,128)(2,1)S(1)})) conditional(s32[]{:T(128)} %bitcast.2, (bf16[384,128]{1,0:T(8,128)(2,1)S(1)}, bf16[128,128]{1,0:T(8,128)(2,1)S(1)}, bf16[256,128]{1,0:T(8,128)(2,1)S(1)}, f32[6,128]{1,0:T(8,128)S(1)}) %tuple.17, ...), branch_computations={%region_0.0_spmd, %region_1.0_spmd, %region_2.0_spmd, %region_3.0_... | conditional | bytes 1179776 | solution.py:452
  8.5 1.6 %collective-permute-start = (bf16[384,128]{1,0:T(8,128)(2,1)S(1)}, bf16[384,128]{1,0:T(8,128)(2,1)S(1)}, u32[]{:S(2)}, u32[]{:S(2)}) collective-permute-start(bf16[384,128]{1,0:T(8,128)(2,1)S(1)} %get-tuple-element.39), channel_id=1, source_target_pairs={{0,6},{2,16},{4,22},{6,0},{8,26},{10,12},{12,10},{14,28},{16,2},{1... | collective-permute-start | bytes 294920 | tf_op jit(solution)/shard_map/cond/branch_0_fun/ppermute | solution.py:354
  10.1 2.5 %collective-permute-done.received = bf16[384,128]{1,0:T(8,128)(2,1)S(1)} collective-permute-done((bf16[384,128]{1,0:T(8,128)(2,1)S(1)}, bf16[384,128]{1,0:T(8,128)(2,1)S(1)}, u32[]{:S(2)}, u32[]{:S(2)}) %collective-permute-start) | collective-permute-done | bytes 98336 | tf_op jit(solution)/shard_map/cond/branch_0_fun/ppermute | solution.py:354
  12.6 3.0 %collective-permute-start.1 = (bf16[384,128]{1,0:T(8,128)(2,1)S(1)}, bf16[384,128]{1,0:T(8,128)(2,1)S(1)}, u32[]{:S(2)}, u32[]{:S(2)}) collective-permute-start(bf16[384,128]{1,0:T(8,128)(2,1)S(1)} %get-tuple-element.43), channel_id=1, source_target_pairs={{0,18},{2,8},{4,14},{6,20},{8,2},{10,24},{12,30},{14,4},{16,26},{1... | collective-permute-start | bytes 294920 | tf_op jit(solution)/shard_map/cond/branch_0_fun/ppermute | solution.py:354
  15.6 2.6 %collective-permute-done.1.received = bf16[384,128]{1,0:T(8,128)(2,1)S(1)} collective-permute-done((bf16[384,128]{1,0:T(8,128)(2,1)S(1)}, bf16[384,128]{1,0:T(8,128)(2,1)S(1)}, u32[]{:S(2)}, u32[]{:S(2)}) %collective-permute-start.1) | collective-permute-done | bytes 98336 | tf_op jit(solution)/shard_map/cond/branch_0_fun/ppermute | solution.py:354
  18.2 1.9 %collective-permute-start.2 = (bf16[384,128]{1,0:T(8,128)(2,1)S(1)}, bf16[384,128]{1,0:T(8,128)(2,1)S(1)}, u32[]{:S(2)}, u32[]{:S(2)}) collective-permute-start(bf16[384,128]{1,0:T(8,128)(2,1)S(1)} %get-tuple-element.46), channel_id=1, source_target_pairs={{0,10},{2,4},{4,2},{6,12},{8,14},{10,0},{12,6},{14,8},{16,22},{18,... | collective-permute-start | bytes 294920 | tf_op jit(solution)/shard_map/cond/branch_0_fun/ppermute | solution.py:354
  20.1 2.3 %collective-permute-done.2.received = bf16[384,128]{1,0:T(8,128)(2,1)S(1)} collective-permute-done((bf16[384,128]{1,0:T(8,128)(2,1)S(1)}, bf16[384,128]{1,0:T(8,128)(2,1)S(1)}, u32[]{:S(2)}, u32[]{:S(2)}) %collective-permute-start.2) | collective-permute-done | bytes 98336 | tf_op jit(solution)/shard_map/cond/branch_0_fun/ppermute | solution.py:354
  22.4 0.1 step3_0.1
  22.5 0.8 %collective-permute-start.14 = (bf16[256,128]{1,0:T(8,128)(2,1)S(1)}, bf16[256,128]{1,0:T(8,128)(2,1)S(1)}, u32[]{:S(2)}, u32[]{:S(2)}) collective-permute-start(bf16[256,128]{1,0:T(8,128)(2,1)S(1)} %get-tuple-element.111), channel_id=1, source_target_pairs={{0,2},{2,0},{4,6},{6,4},{8,10},{10,8},{12,14},{14,12},{16,18},{18,... | collective-permute-start | bytes 196616 | tf_op jit(solution)/shard_map/ppermute | solution.py:354
  23.3 0.5 %own.1.before = f32[128,512]{1,0:T(8,128)S(1)} custom-call(bf16[512,512]{1,0:T(8,128)(2,1)S(1)} %get-tuple-element.115.local_high, bf16[512,512]{1,0:T(8,128)(2,1)S(1)} %get-tuple-element.116.local_low, bf16[128,512]{1,0:T(8,128)(2,1)S(1)} %get-tuple-element.105.projected, bf16[128,256]{1,0:T(8,128)(2,1)S(1)} %get-tuple-element.117.weight, ...), custom_call_target="tpu_custom_call" | custom-call | flops 167772160 | bytes 2097152 | tf_op jit(solution)/shard_map/own/pallas_call | solution.py:458
  23.8 0.5 %far.1.before = f32[128,512]{1,0:T(8,128)S(1)} custom-call(bf16[512,512]{1,0:T(8,128)(2,1)S(1)} %get-tuple-element.112.high, bf16[512,512]{1,0:T(8,128)(2,1)S(1)} %get-tuple-element.113.low, bf16[512,128]{1,0:T(8,128)(2,1)S(1)} %get-tuple-element.114.near, f32[128,512]{1,0:T(8,128)S(1)} %own.1.before), custom_call_target="tpu_custom_call" | custom-call | flops 134217728 | bytes 2097152 | tf_op jit(solution)/shard_map/far/pallas_call | solution.py:459
  24.3 0.0 collective-permute-done.14.theirs
  24.3 0.9 %finish.1 = bf16[128,512]{1,0:T(8,128)(2,1)} custom-call(bf16[256,512]{1,0:T(8,128)(2,1)S(1)} %get-tuple-element.98.high, bf16[256,512]{1,0:T(8,128)(2,1)S(1)} %get-tuple-element.99.low, bf16[256,128]{1,0:T(8,128)(2,1)S(1)} %collective-permute-done.14.theirs, f32[128,512]{1,0:T(8,128)S(1)} %far.1.before), custom_call_target="tpu_custom_call" | custom-call | bytes 1048576 | tf_op jit(solution)/shard_map/finish/pallas_call | solution.py:463
  (2 shorter events, 0.1 us)
Async XLA Ops:
  0.0 6.6 %collective-permute-start.12 = (bf16[128,512]{1,0:T(8,128)(2,1)}, bf16[128,512]{1,0:T(8,128)(2,1)S(1)}, u32[]{:S(2)}, u32[]{:S(2)}) collective-permute-start(bf16[128,512]{1,0:T(8,128)(2,1)} %refs_14_.1), channel_id=1, source_target_pairs={{0,1},{1,0},{2,3},{3,2},{4,5},{5,4},{6,7},{7,6},{8,9},{9,8},{10,11... | collective-permute-start | bytes 393224 | tf_op jit(solution)/shard_map/ppermute | solution.py:357
  7.0 1.4 %collective-permute-start.13 = (bf16[384,128]{1,0:T(8,128)(2,1)S(1)}, bf16[384,128]{1,0:T(8,128)(2,1)S(1)}, u32[]{:S(2)}, u32[]{:S(2)}) collective-permute-start(bf16[384,128]{1,0:T(8,128)(2,1)S(1)} %get-tuple-element.106), channel_id=1, source_target_pairs={{0,2},{2,0},{4,6},{6,4},{8,10},{10,8},{12,14},{14,12},{16,18},{18,... | collective-permute-start | bytes 294920 | tf_op jit(solution)/shard_map/ppermute | solution.py:354
  8.5 4.1 %collective-permute-start = (bf16[384,128]{1,0:T(8,128)(2,1)S(1)}, bf16[384,128]{1,0:T(8,128)(2,1)S(1)}, u32[]{:S(2)}, u32[]{:S(2)}) collective-permute-start(bf16[384,128]{1,0:T(8,128)(2,1)S(1)} %get-tuple-element.39), channel_id=1, source_target_pairs={{0,6},{2,16},{4,22},{6,0},{8,26},{10,12},{12,10},{14,28},{16,2},{1... | collective-permute-start | bytes 294920 | tf_op jit(solution)/shard_map/cond/branch_0_fun/ppermute | solution.py:354
  12.6 5.6 %collective-permute-start.1 = (bf16[384,128]{1,0:T(8,128)(2,1)S(1)}, bf16[384,128]{1,0:T(8,128)(2,1)S(1)}, u32[]{:S(2)}, u32[]{:S(2)}) collective-permute-start(bf16[384,128]{1,0:T(8,128)(2,1)S(1)} %get-tuple-element.43), channel_id=1, source_target_pairs={{0,18},{2,8},{4,14},{6,20},{8,2},{10,24},{12,30},{14,4},{16,26},{1... | collective-permute-start | bytes 294920 | tf_op jit(solution)/shard_map/cond/branch_0_fun/ppermute | solution.py:354
  18.2 4.2 %collective-permute-start.2 = (bf16[384,128]{1,0:T(8,128)(2,1)S(1)}, bf16[384,128]{1,0:T(8,128)(2,1)S(1)}, u32[]{:S(2)}, u32[]{:S(2)}) collective-permute-start(bf16[384,128]{1,0:T(8,128)(2,1)S(1)} %get-tuple-element.46), channel_id=1, source_target_pairs={{0,10},{2,4},{4,2},{6,12},{8,14},{10,0},{12,6},{14,8},{16,22},{18,... | collective-permute-start | bytes 294920 | tf_op jit(solution)/shard_map/cond/branch_0_fun/ppermute | solution.py:354
  22.5 1.8 %collective-permute-start.14 = (bf16[256,128]{1,0:T(8,128)(2,1)S(1)}, bf16[256,128]{1,0:T(8,128)(2,1)S(1)}, u32[]{:S(2)}, u32[]{:S(2)}) collective-permute-start(bf16[256,128]{1,0:T(8,128)(2,1)S(1)} %get-tuple-element.111), channel_id=1, source_target_pairs={{0,2},{2,0},{4,6},{6,4},{8,10},{10,8},{12,14},{14,12},{16,18},{18,... | collective-permute-start | bytes 196616 | tf_op jit(solution)/shard_map/ppermute | solution.py:354
where the time goes:
time: 25.4 us; the launch traced here: 25.2 us
  starting transfers between devices  10.3 us (41%)
  waiting for transfers between devices  8.41 us (33%)
  Pallas kernels  5.78 us (23%)
  between operations  0.72 us (3%)
    ppermute x5, waiting for transfers between devices, swap(): return lax.ppermute(x, 'dom', partners(parts, k))  7.78 us
    ppermute x5, starting transfers between devices, swap(): return lax.ppermute(x, 'dom', partners(parts, k))  7.33 us
    pallas_call x1, Pallas kernels, shards(): call(functools.partial(prepare, 2 * border // tile), (like(2 * (border +...  3.07 us
    ppermute x1, starting transfers between devices, shards(): lax.ppermute(features, 'feat', [(0, 1), (1, 0)])  2.94 us
    pallas_call x1, Pallas kernels, shards(): call(finish, like(width, vertices), [VM] * 4, size=1 << 20, name='finish')  0.92 us
    ppermute x1, waiting for transfers between devices, shards(): lax.ppermute(features, 'feat', [(0, 1), (1, 0)])  0.62 us
  transfers between devices with their start and end apart: 6, of which 5 were waited for; matrix products, arithmetic and copies ran while one was open for 0% of the time, Pallas kernels for 17%

commit v1 on v0

--- a/solution.py
+++ b/solution.py
@@ -303,7 +303,9 @@
         brief[border:, :] = sum(merged[i * tile : (i + 1) * tile] for i in range(pairs))
 
 
-def own_terms(local_high, local_low, projected, weight, begun, features, total):
+def known_terms(
+    local_high, local_low, projected, weight, begun, features, high, low, near, total
+):
     width = features.shape[0]
     if begun.shape[0] == 1:
         rest = dot(weight[...], features[...]) + column(begun[...])
@@ -314,12 +316,6 @@
         rest
         + dot(projected[...], local_high[...], LAST)
         + dot(projected[...], local_low[...], LAST)
-    )
-
-
-def far_terms(high, low, near, before, total):
-    total[...] = (
-        before[...]
         + dot(near[...], high[...], FIRST_LAST)
         + dot(near[...], low[...], FIRST_LAST)
     )
@@ -416,13 +412,6 @@
         remain, like(border + hub, width), [VM] * 2, size=1 << 20, name="remain"
     )(projected, choice)
     begun = early[2] if early else bias
-    own = functools.partial(
-        call(
-            own_terms, like(width, vertices, kind=F32), [VM] * 6,
-            flops=4 * vertices * width * (near_size + width), size=2 << 20, name="own",
-        ),
-        local_high, local_low, projected, near_weight, begun, feature_blocks[-1],
-    )
     keep, message, held, brief = call(
         functools.partial(step, 0, parts, cap, False, False, None),
         (like(border, width), like(border + hub, width), like(hub, width), like(border + tile, width)),
@@ -455,11 +444,13 @@
         keep, message, held, brief, marks,
     )
     theirs = swap(message, 0)
-    total = own()
     total = call(
-        far_terms, like(width, vertices, kind=F32), [VM] * 4,
-        flops=4 * vertices * width * (far_size - hub), size=2 << 20, name="far",
-    )(far_high, far_low, keep, total)
+        known_terms, like(width, vertices, kind=F32), [VM] * 9,
+        flops=4 * vertices * width * (near_size + far_size), size=4 << 20, name="known",
+    )(
+        local_high, local_low, projected, near_weight, early[2] if early else bias,
+        feature_blocks[-1], far_high, far_low, keep,
+    )
     return call(finish, like(width, vertices), [VM] * 4, size=1 << 20, name="finish")(
         late_high, late_low, theirs, total
     )

time: 25.4 us -> 23.9 us (0.941)
  waiting for transfers between devices: 8.41 us -> 7.6 us
  starting transfers between devices: 10.3 us -> 9.92 us
    ppermute x5, waiting for transfers between devices: 7.78 us -> 6.97 us  [swap(): return lax.ppermute(x, 'dom', partners(parts, k))]
    ppermute x5, starting transfers between devices: 7.33 us -> 6.98 us  [swap(): return lax.ppermute(x, 'dom', partners(parts, k))]
    pallas_call x2 -> x1, Pallas kernels: 0.98 us -> 0.83 us  [shards(): call(known_terms, like(width, vertices, kind=F32), [VM] * 9, flops=4 * ve...]
  transfers between devices with their start and end apart: 6 -> 6, of which waited for: 5 -> 6; matrix products, arithmetic and copies ran while one was open for 0% -> 0% of each run, Pallas kernels for 17% -> 17%
where the time goes in v1:
time: 23.9 us
  starting transfers between devices  9.92 us (42%)
  waiting for transfers between devices  7.6 us (32%)
  Pallas kernels  5.64 us (24%)
  between operations  0.7 us (3%)
    ppermute x5, starting transfers between devices, swap(): return lax.ppermute(x, 'dom', partners(parts, k))  6.98 us
    ppermute x5, waiting for transfers between devices, swap(): return lax.ppermute(x, 'dom', partners(parts, k))  6.97 us
    pallas_call x1, Pallas kernels, shards(): call(functools.partial(prepare, 2 * border // tile), (like(2 * (border +...  3.07 us
    ppermute x1, starting transfers between devices, shards(): lax.ppermute(features, 'feat', [(0, 1), (1, 0)])  2.94 us
    pallas_call x1, Pallas kernels, shards(): call(finish, like(width, vertices), [VM] * 4, size=1 << 20, name='finish')  0.91 us
    pallas_call x1, Pallas kernels, shards(): call(known_terms, like(width, vertices, kind=F32), [VM] * 9, flops=4 * ve...  0.83 us
    ppermute x1, waiting for transfers between devices, shards(): lax.ppermute(features, 'feat', [(0, 1), (1, 0)])  0.62 us
  transfers between devices with their start and end apart: 6, of which 6 were waited for; matrix products, arithmetic and copies ran while one was open for 0% of the time, Pallas kernels for 17%

profile of v1, /device:TPU:0, one launch (start us, length us, event | category | flops | bytes accessed | tf_op | source)
XLA Modules:
  0.0 23.9 jit_solution(9662935549127935092)
XLA Ops:
  0.0 2.9 %collective-permute-start.12 = (bf16[128,512]{1,0:T(8,128)(2,1)}, bf16[128,512]{1,0:T(8,128)(2,1)S(1)}, u32[]{:S(2)}, u32[]{:S(2)}) collective-permute-start(bf16[128,512]{1,0:T(8,128)(2,1)} %refs_14_.1), channel_id=1, source_target_pairs={{0,1},{1,0},{2,3},{3,2},{4,5},{5,4},{6,7},{7,6},{8,9},{9,8},{10,11... | collective-permute-start | bytes 393224 | tf_op jit(solution)/shard_map/ppermute | solution.py:353
  2.9 3.1 %prepare.1 = (bf16[768,512]{1,0:T(8,128)(2,1)S(1)}, f32[6,128]{1,0:T(8,128)S(1)}, s32[1]{0:T(128)}, bf16[128,256]{1,0:T(8,128)(2,1)S(1)}, f32[1,128]{1,0:T(1,128...) custom-call(s32[4]{0:T(128)} %refs_0_.1, ...), custom_call_target="tpu_custom_call" | custom-call | bytes 8388608 | tf_op jit(solution)/shard_map/prepare/pallas_call | solution.py:372
  6.0 0.6 %collective-permute-done.12.features = bf16[128,512]{1,0:T(8,128)(2,1)S(1)} collective-permute-done((bf16[128,512]{1,0:T(8,128)(2,1)}, bf16[128,512]{1,0:T(8,128)(2,1)S(1)}, u32[]{:S(2)}, u32[]{:S(2)}) %collective-permute-start.12) | collective-permute-done | bytes 131104 | tf_op jit(solution)/shard_map/ppermute | solution.py:353
  6.6 0.4 %pick.1 = (bf16[128,512]{1,0:T(8,128)(2,1)S(1)}, bf16[384,128]{1,0:T(8,128)(2,1)S(1)}) custom-call(bf16[128,128]{1,0:T(8,128)(2,1)S(1)} %get-tuple-element.101.weight, bf16[128,512]{1,0:T(8,128)(2,1)S(1)} %collective-permute-done.12.features, bf16[768,512]{1,0:T(8,128)(2,1)S(1)} %get-tuple-element.102.choice, f32[128,512]{1,0:T(8,128)S(1)} %get-tuple-element.103.refs_0_, ...), custom_call_target="tpu_custom_call" | custom-call | bytes 1048576 | tf_op jit(solution)/shard_map/pick/pallas_call | solution.py:406
  7.0 0.1 collective-permute-start.13
  7.8 0.3 %remain.1.keep.hub = bf16[384,128]{1,0:T(8,128)(2,1)S(1)} custom-call(bf16[128,512]{1,0:T(8,128)(2,1)S(1)} %get-tuple-element.105.projected, bf16[768,512]{1,0:T(8,128)(2,1)S(1)} %get-tuple-element.102.choice), custom_call_target="tpu_custom_call" | custom-call | bytes 1048576 | tf_op jit(solution)/shard_map/remain/pallas_call | solution.py:411
  8.0 0.4 %collective-permute-done.13.received = bf16[384,128]{1,0:T(8,128)(2,1)S(1)} collective-permute-done((bf16[384,128]{1,0:T(8,128)(2,1)S(1)}, bf16[384,128]{1,0:T(8,128)(2,1)S(1)}, u32[]{:S(2)}, u32[]{:S(2)}) %collective-permute-start.13) | collective-permute-done | bytes 98336 | tf_op jit(solution)/shard_map/ppermute | solution.py:350
  8.4 0.1 step0.1
  8.5 13.2 %conditional.1 = ((bf16[512,128]{1,0:T(8,128)(2,1)S(1)}, bf16[256,128]{1,0:T(8,128)(2,1)S(1)})) conditional(s32[]{:T(128)} %bitcast.2, (bf16[384,128]{1,0:T(8,128)(2,1)S(1)}, bf16[128,128]{1,0:T(8,128)(2,1)S(1)}, bf16[256,128]{1,0:T(8,128)(2,1)S(1)}, f32[6,128]{1,0:T(8,128)S(1)}) %tuple.17, ...), branch_computations={%region_0.0_spmd, %region_1.0_spmd, %region_2.0_spmd, %region_3.0_... | conditional | bytes 1179776 | solution.py:441
  8.5 1.6 %collective-permute-start.6 = (bf16[256,128]{1,0:T(8,128)(2,1)S(1)}, bf16[256,128]{1,0:T(8,128)(2,1)S(1)}, u32[]{:S(2)}, u32[]{:S(2)}) collective-permute-start(bf16[256,128]{1,0:T(8,128)(2,1)S(1)} %get-tuple-element.59), channel_id=1, source_target_pairs={{0,6},{2,16},{4,22},{6,0},{8,26},{10,12},{12,10},{14,28},{16,2},{1... | collective-permute-start | bytes 196616 | tf_op jit(solution)/shard_map/cond/branch_2_fun/ppermute | solution.py:350
  10.1 2.2 %collective-permute-done.6.received = bf16[256,128]{1,0:T(8,128)(2,1)S(1)} collective-permute-done((bf16[256,128]{1,0:T(8,128)(2,1)S(1)}, bf16[256,128]{1,0:T(8,128)(2,1)S(1)}, u32[]{:S(2)}, u32[]{:S(2)}) %collective-permute-start.6) | collective-permute-done | bytes 65568 | tf_op jit(solution)/shard_map/cond/branch_2_fun/ppermute | solution.py:350
  12.3 3.0 %collective-permute-start.7 = (bf16[256,128]{1,0:T(8,128)(2,1)S(1)}, bf16[256,128]{1,0:T(8,128)(2,1)S(1)}, u32[]{:S(2)}, u32[]{:S(2)}) collective-permute-start(bf16[256,128]{1,0:T(8,128)(2,1)S(1)} %get-tuple-element.63), channel_id=1, source_target_pairs={{0,18},{2,8},{4,14},{6,20},{8,2},{10,24},{12,30},{14,4},{16,26},{1... | collective-permute-start | bytes 196616 | tf_op jit(solution)/shard_map/cond/branch_2_fun/ppermute | solution.py:350
  15.3 2.0 %collective-permute-done.7.received = bf16[256,128]{1,0:T(8,128)(2,1)S(1)} collective-permute-done((bf16[256,128]{1,0:T(8,128)(2,1)S(1)}, bf16[256,128]{1,0:T(8,128)(2,1)S(1)}, u32[]{:S(2)}, u32[]{:S(2)}) %collective-permute-start.7) | collective-permute-done | bytes 65568 | tf_op jit(solution)/shard_map/cond/branch_2_fun/ppermute | solution.py:350
  17.3 2.0 %collective-permute-start.8 = (bf16[384,128]{1,0:T(8,128)(2,1)S(1)}, bf16[384,128]{1,0:T(8,128)(2,1)S(1)}, u32[]{:S(2)}, u32[]{:S(2)}) collective-permute-start(bf16[384,128]{1,0:T(8,128)(2,1)S(1)} %get-tuple-element.66), channel_id=1, source_target_pairs={{0,10},{2,4},{4,2},{6,12},{8,14},{10,0},{12,6},{14,8},{16,22},{18,... | collective-permute-start | bytes 294920 | tf_op jit(solution)/shard_map/cond/branch_2_fun/ppermute | solution.py:350
  19.3 2.3 %collective-permute-done.8.received = bf16[384,128]{1,0:T(8,128)(2,1)S(1)} collective-permute-done((bf16[384,128]{1,0:T(8,128)(2,1)S(1)}, bf16[384,128]{1,0:T(8,128)(2,1)S(1)}, u32[]{:S(2)}, u32[]{:S(2)}) %collective-permute-start.8) | collective-permute-done | bytes 98336 | tf_op jit(solution)/shard_map/cond/branch_2_fun/ppermute | solution.py:350
  21.6 0.1 step3_2.1
  21.7 0.3 %collective-permute-start.14 = (bf16[256,128]{1,0:T(8,128)(2,1)S(1)}, bf16[256,128]{1,0:T(8,128)(2,1)S(1)}, u32[]{:S(2)}, u32[]{:S(2)}) collective-permute-start(bf16[256,128]{1,0:T(8,128)(2,1)S(1)} %get-tuple-element.111), channel_id=1, source_target_pairs={{0,2},{2,0},{4,6},{6,4},{8,10},{10,8},{12,14},{14,12},{16,18},{18,... | collective-permute-start | bytes 196616 | tf_op jit(solution)/shard_map/ppermute | solution.py:350
  22.0 0.8 %known.1.before = f32[128,512]{1,0:T(8,128)S(1)} custom-call(bf16[512,512]{1,0:T(8,128)(2,1)S(1)} %get-tuple-element.112.local_high, bf16[512,512]{1,0:T(8,128)(2,1)S(1)} %get-tuple-element.113.local_low, bf16[128,512]{1,0:T(8,128)(2,1)S(1)} %get-tuple-element.105.projected, bf16[128,256]{1,0:T(8,128)(2,1)S(1)} %get-tuple-element.114.weight, ...), custom_call_target="tpu_custom_call" | custom-call | flops 335544320 | bytes 4194304 | tf_op jit(solution)/shard_map/known/pallas_call | solution.py:447
  22.8 0.1 collective-permute-done.14.theirs
  23.0 0.9 %finish.1 = bf16[128,512]{1,0:T(8,128)(2,1)} custom-call(bf16[256,512]{1,0:T(8,128)(2,1)S(1)} %get-tuple-element.98.high, bf16[256,512]{1,0:T(8,128)(2,1)S(1)} %get-tuple-element.99.low, bf16[256,128]{1,0:T(8,128)(2,1)S(1)} %collective-permute-done.14.theirs, f32[128,512]{1,0:T(8,128)S(1)} %known.1.before), custom_call_target="tpu_custom_call" | custom-call | bytes 1048576 | tf_op jit(solution)/shard_map/finish/pallas_call | solution.py:454
  (2 shorter events, 0.1 us)
Async XLA Ops:
  0.0 6.6 %collective-permute-start.12 = (bf16[128,512]{1,0:T(8,128)(2,1)}, bf16[128,512]{1,0:T(8,128)(2,1)S(1)}, u32[]{:S(2)}, u32[]{:S(2)}) collective-permute-start(bf16[128,512]{1,0:T(8,128)(2,1)} %refs_14_.1), channel_id=1, source_target_pairs={{0,1},{1,0},{2,3},{3,2},{4,5},{5,4},{6,7},{7,6},{8,9},{9,8},{10,11... | collective-permute-start | bytes 393224 | tf_op jit(solution)/shard_map/ppermute | solution.py:353
  7.0 1.4 %collective-permute-start.13 = (bf16[384,128]{1,0:T(8,128)(2,1)S(1)}, bf16[384,128]{1,0:T(8,128)(2,1)S(1)}, u32[]{:S(2)}, u32[]{:S(2)}) collective-permute-start(bf16[384,128]{1,0:T(8,128)(2,1)S(1)} %get-tuple-element.106), channel_id=1, source_target_pairs={{0,2},{2,0},{4,6},{6,4},{8,10},{10,8},{12,14},{14,12},{16,18},{18,... | collective-permute-start | bytes 294920 | tf_op jit(solution)/shard_map/ppermute | solution.py:350
  8.5 3.8 %collective-permute-start.6 = (bf16[256,128]{1,0:T(8,128)(2,1)S(1)}, bf16[256,128]{1,0:T(8,128)(2,1)S(1)}, u32[]{:S(2)}, u32[]{:S(2)}) collective-permute-start(bf16[256,128]{1,0:T(8,128)(2,1)S(1)} %get-tuple-element.59), channel_id=1, source_target_pairs={{0,6},{2,16},{4,22},{6,0},{8,26},{10,12},{12,10},{14,28},{16,2},{1... | collective-permute-start | bytes 196616 | tf_op jit(solution)/shard_map/cond/branch_2_fun/ppermute | solution.py:350
  12.3 5.0 %collective-permute-start.7 = (bf16[256,128]{1,0:T(8,128)(2,1)S(1)}, bf16[256,128]{1,0:T(8,128)(2,1)S(1)}, u32[]{:S(2)}, u32[]{:S(2)}) collective-permute-start(bf16[256,128]{1,0:T(8,128)(2,1)S(1)} %get-tuple-element.63), channel_id=1, source_target_pairs={{0,18},{2,8},{4,14},{6,20},{8,2},{10,24},{12,30},{14,4},{16,26},{1... | collective-permute-start | bytes 196616 | tf_op jit(solution)/shard_map/cond/branch_2_fun/ppermute | solution.py:350
  17.3 4.3 %collective-permute-start.8 = (bf16[384,128]{1,0:T(8,128)(2,1)S(1)}, bf16[384,128]{1,0:T(8,128)(2,1)S(1)}, u32[]{:S(2)}, u32[]{:S(2)}) collective-permute-start(bf16[384,128]{1,0:T(8,128)(2,1)S(1)} %get-tuple-element.66), channel_id=1, source_target_pairs={{0,10},{2,4},{4,2},{6,12},{8,14},{10,0},{12,6},{14,8},{16,22},{18,... | collective-permute-start | bytes 294920 | tf_op jit(solution)/shard_map/cond/branch_2_fun/ppermute | solution.py:350
  21.7 1.3 %collective-permute-start.14 = (bf16[256,128]{1,0:T(8,128)(2,1)S(1)}, bf16[256,128]{1,0:T(8,128)(2,1)S(1)}, u32[]{:S(2)}, u32[]{:S(2)}) collective-permute-start(bf16[256,128]{1,0:T(8,128)(2,1)S(1)} %get-tuple-element.111), channel_id=1, source_target_pairs={{0,2},{2,0},{4,6},{6,4},{8,10},{10,8},{12,14},{14,12},{16,18},{18,... | collective-permute-start | bytes 196616 | tf_op jit(solution)/shard_map/ppermute | solution.py:350
